TPU v7x, 32 devices: a whole 2x2x4 slice. The times are simulated.
32 devices in a mesh: samp: 8 (over z, y), feat: 4 (over x, core).
Axes of the slice: x: 2, y: 2, z: 4, core: 2. Of those that a mesh axis runs over, the one named last changes fastest.
Arguments:
- data: bfloat16 [8192, 4096], P('samp', 'feat'), may hold values from -0.09375 to 0.09375
- targets: float32 [8192, 256], P('samp'), may hold values from -24 to 24
- tile_x: float32 [8, 4096, 256], P('samp', 'feat'), may hold values from -6 to 6
- x_dual: float32 [8, 4096, 256], P('samp', 'feat'), may hold values from -6 to 6
- tile_y: float32 [4, 8192, 256], P('feat', 'samp'), may hold values from -6 to 6
- y_dual: float32 [4, 8192, 256], P('feat', 'samp'), may hold values from -6 to 6
Outputs:
- new_x: float32 [8, 4096, 256], P('samp', 'feat')
- new_x_dual: float32 [8, 4096, 256], P('samp', 'feat')
- new_y: float32 [4, 8192, 256], P('feat', 'samp')
- new_y_dual: float32 [4, 8192, 256], P('feat', 'samp')
All inputs are finite; a program needn't handle non-finite values.
Results may differ from a plain program's by a relative error of at most 0.0041.
Values sent between devices are 32-bit elements; how exact they have to be, the bound alone decides.
A program may use at most 128 MiB of HBM per device.

v0:
```python
import jax
import jax.numpy as jnp
from jax import lax
from jax.sharding import PartitionSpec as P

ITERS = 2
huber_width = 0.5
shrink_level = 0.1
f32 = jnp.float32
bf16 = jnp.bfloat16


def soft_shrink(values):
    return jnp.sign(values) * jnp.maximum(jnp.abs(values) - shrink_level, 0.0)


def huber_prox(values, weight):
    limit = huber_width * (1.0 + weight)
    return jnp.where(
        jnp.abs(values) <= limit,
        values / (1.0 + weight),
        values - weight * huber_width * jnp.sign(values),
    )


def dot(a, b):
    return jnp.dot(a, b, preferred_element_type=f32)


def shards(data, targets, tile_x, x_dual, tile_y, y_dual):
    n_samp = lax.axis_size("samp")
    n_feat = lax.axis_size("feat")
    order = data.shape[0]
    q = tile_x[0] + x_dual[0]
    p = tile_y[0] + y_dual[0]
    gram = lax.dot_general(data, data, (((1,), (1,)), ((), ())), preferred_element_type=f32)
    identity = jnp.eye(order, dtype=f32)
    wide = data.astype(f32)
    factor = 1.0 / (1.0 + 2.0 * jnp.sum(wide * wide) / order)
    a = 2.0 * factor - factor * factor
    b = factor * factor
    g16 = gram.astype(bf16)
    inner = (2.0 - a) * identity + (b - a) * gram + b * dot(g16, g16)
    inverse = a * inner - b * dot(g16, inner.astype(bf16))
    back_map = lax.dot_general(
        data, inverse.astype(bf16), (((0,), (0,)), ((), ())), preferred_element_type=f32
    ).astype(bf16)
    for turn_index in range(ITERS):
        consensus = soft_shrink(lax.psum(q, "samp") / n_samp)
        total = lax.psum(p, "feat")
        correction = (targets + huber_prox(total - targets, float(n_feat)) - total) / n_feat
        dual = q - consensus
        start = consensus - dual
        aim = p + 2.0 * correction
        ahead = dot(data, start.astype(bf16))
        back = dot(back_map, (ahead - aim).astype(bf16))
        coeffs = start - back
        partials = ahead - dot(data, back.astype(bf16))
        q = consensus - back
        p = partials - correction
    return (coeffs[None], dual[None], partials[None], -correction[None])


def solution(mesh):
    return jax.shard_map(
        shards,
        mesh=mesh,
        in_specs=(
            P("samp", "feat"),
            P("samp", None),
            P("samp", "feat", None),
            P("samp", "feat", None),
            P("feat", "samp", None),
            P("feat", "samp", None),
        ),
        out_specs=(
            P("samp", "feat", None),
            P("samp", "feat", None),
            P("feat", "samp", None),
            P("feat", "samp", None),
        ),
        check_vma=False,
    )
```

profile of v0, /device:TPU:0, one launch (start us, length us, event | category | flops | bytes accessed | tf_op | source)
XLA Modules:
  0.0 277.3 jit_solution(14655936725483755482)
XLA Ops:
  7.2 0.0 copy-start.10
  7.2 0.0 all-reduce.5.cloned.1.call-start
  7.2 2.7 add_bitcast_fusion.1
  9.9 0.0 copy-start.11
  9.9 0.0 all-reduce.5.cloned.1.call-update
  10.0 0.0 all-reduce.7.cloned.1.call-start
  10.0 0.0 copy-done.10
  10.0 0.3 copy.10
  10.4 0.8 copy-done.11
  11.2 1.3 copy.11
  12.5 0.0 copy-start
  12.5 2.5 add_bitcast_fusion
  15.0 0.0 all-reduce.7.cloned.1.call-update
  15.0 0.0 all-reduce.11.cloned.1.call-start
  15.0 0.0 copy-done
  15.0 1.7 multiply_reduce_fusion
  17.4 2.4 fusion.34
  19.8 0.0 copy-start.12
  19.8 2.0 copy-done.12
  21.8 4.3 %multiply_add_fusion = f32[1024,1024]{1,0:T(8,128)} fusion(f32[1024,1024]{1,0:T(8,128)S(1)} %fusion.34, f32[]{:T(128)S(6)} %mul.62, f32[]{:T(128)S(6)} %sub.72, f32[]{:T(128)S(6)} %sub.71), kind=kOutput, calls=%fused_computation.1 | convolution fusion | flops 2154823680 | bytes 8388620 | tf_op jit(solution)/shard_map/dot_general | solution.py:27
  26.1 10.7 %convolution_convert_fusion = bf16[1024,1024]{1,0:T(8,128)(2,1)} fusion(bf16[1024,1024]{1,0:T(8,128)(2,1)S(1)} %copy-done, f32[1024,1024]{1,0:T(8,128)} %multiply_add_fusion, f32[]{:T(128)S(6)} %mul.62, f32[]{:T(128)S(6)} %sub.70, f32[1024,1024]{1,0:T(8,128)} %copy-done.12), kind=kOutput, calls=%fused_computation.5 | convolution fusion | flops 4302307328 | bytes 12582920 | tf_op jit(solution)/shard_map/dot_general | solution.py:45
  36.8 1.6 copy.13
  38.3 54.8 %all-reduce.5.cloned.1.call-done = f32[1024,256]{1,0:T(8,128)} async-done(((f32[1024,256]{1,0:T(8,128)}), f32[1024,256]{1,0:T(8,128)}) %all-reduce.5.cloned.1.call-update) | async-done | bytes 1048592 | tf_op jit(solution)/shard_map/psum | solution.py:49
  93.2 3.7 %convolution_bitcast_fusion.3 = f32[1024,256]{0,1:T(8,128)} fusion(bf16[1024,1024]{1,0:T(8,128)(2,1)S(1)} %copy-done, f32[1024,256]{1,0:T(8,128)} %add_bitcast_fusion.1, f32[1024,256]{1,0:T(8,128)} %all-reduce.5.cloned.1.call-done), kind=kOutput, calls=%fused_computation.10 | convolution fusion | flops 539230208 | bytes 5242880 | tf_op jit(solution)/shard_map/dot_general | solution.py:27
  96.8 35.2 %all-reduce.7.cloned.1.call-done = f32[1024,256]{0,1:T(8,128)} async-done(((f32[1024,256]{0,1:T(8,128)}), f32[1024,256]{0,1:T(8,128)}) %all-reduce.7.cloned.1.call-update) | async-done | bytes 1048592 | tf_op jit(solution)/shard_map/psum | solution.py:50
  132.0 0.0 copy-start.5
  132.0 0.0 copy-start.9
  132.0 5.3 %fusion.14 = (f32[1024,256]{1,0:T(8,128)}, bf16[1024,256]{1,0:T(8,128)(2,1)S(1)}) fusion(f32[1024,256]{1,0:T(8,128)} %all-reduce.5.cloned.1.call-done, bf16[1024,1024]{1,0:T(8,128)(2,1)} %convolution_convert_fusion, f32[1024,256]{0,1:T(8,128)} %convolution_bitcast_fusion.3, f32[1024,256]{0,1:T(8,128)} %add_bitcast_fusion, ...), kind=kOutput, calls=%fused_computation.34 | convolution fusion | flops 542638080 | bytes 8912896 | tf_op jit(solution)/shard_map/dot_general | solution.py:27
  137.3 0.0 copy-done.5
  137.3 0.0 copy-done.9
  137.3 2.4 fusion.2
  139.8 0.0 all-reduce.11.cloned.1.call-update
  139.8 0.0 all-reduce.9.cloned.1.call-start
  139.8 0.5 all-reduce.9.cloned.1.call-update
  140.4 36.4 %all-reduce.11.cloned.1.call-done = f32[1024,256]{0,1:T(8,128)} async-done(((f32[1024,256]{0,1:T(8,128)}), f32[1024,256]{0,1:T(8,128)}) %all-reduce.11.cloned.1.call-update) | async-done | bytes 1048592 | tf_op jit(solution)/shard_map/psum | solution.py:50
  176.7 2.8 %negate_bitcast_fusion = f32[1,1024,256]{1,2,0:T(8,128)} fusion(f32[1024,256]{0,1:T(8,128)} %all-reduce.11.cloned.1.call-done, f32[1024,256]{0,1:T(8,128)S(1)} %copy.13), kind=kLoop, calls=%fused_computation.16 | loop fusion | flops 3145728 | bytes 3145728 | tf_op jit(solution)/shard_map/neg | solution.py:61
  179.5 2.5 copy.17
  182.0 77.4 %all-reduce.9.cloned.1.call-done = f32[1024,256]{1,0:T(8,128)} async-done(((f32[1024,256]{1,0:T(8,128)}), f32[1024,256]{1,0:T(8,128)}) %all-reduce.9.cloned.1.call-update) | async-done | bytes 1048592 | tf_op jit(solution)/shard_map/psum | solution.py:49
  259.5 0.0 copy-start.2
  259.5 0.0 copy-start.6
  259.5 0.0 copy-start.7
  259.5 2.8 %convolution_bitcast_fusion.2 = f32[1024,256]{0,1:T(8,128)S(1)} fusion(bf16[1024,1024]{1,0:T(8,128)(2,1)S(1)} %copy-done, f32[1024,256]{1,0:T(8,128)} %get-tuple-element.10, f32[1024,256]{1,0:T(8,128)} %all-reduce.9.cloned.1.call-done), kind=kOutput, calls=%fused_computation.9 | convolution fusion | flops 539230208 | bytes 5242880 | tf_op jit(solution)/shard_map/dot_general | solution.py:27
  262.3 0.0 copy-done.2
  262.3 0.0 copy-done.6
  262.3 0.0 copy-done.7
  262.3 1.2 fusion.16
  263.5 0.0 copy-start.3
  263.5 1.0 copy-done.3
  264.5 0.0 copy-start.8
  264.5 1.8 fusion.4
  266.3 0.0 copy-start.1
  266.3 0.0 copy-start.4
  266.3 2.7 copy.16
  269.0 0.0 copy-done.8
  269.0 0.0 copy-done.1
  269.0 0.0 copy-done.4
  269.0 1.8 subtract_bitcast_fusion.1
Async XLA Ops:
  7.2 2.9 %copy-start.10 = (f32[1,1024,256]{2,1,0:T(8,128)S(1)}, f32[1,1024,256]{2,1,0:T(8,128)}, u32[]{:S(2)}) copy-start(f32[1,1024,256]{2,1,0:T(8,128)} %param.10) | copy-start | bytes 3145732
  7.2 86.0 %all-reduce.5.cloned.1.call-start = ((), (), s32[]{:S(2)}) async-start(), calls=%async_computation | async-start | bytes 2097152 | tf_op jit(solution)/shard_map/psum | solution.py:49
  9.9 1.2 copy-start.11
  10.0 122.1 %all-reduce.7.cloned.1.call-start = ((), (), s32[]{:S(2)}) async-start(), calls=%async_computation.1 | async-start | bytes 2097152 | tf_op jit(solution)/shard_map/psum | solution.py:50
  12.5 2.6 copy-start
  15.0 161.7 %all-reduce.11.cloned.1.call-start = ((), (), s32[]{:S(2)}) async-start(), calls=%async_computation.3 | async-start | bytes 2097152 | tf_op jit(solution)/shard_map/psum | solution.py:50
  19.8 2.0 copy-start.12
  132.0 5.3 %copy-start.5 = (f32[1024,256]{0,1:T(8,128)S(1)}, f32[1024,256]{0,1:T(8,128)}, u32[]{:S(2)}) copy-start(f32[1024,256]{0,1:T(8,128)} %convolution_bitcast_fusion.3) | copy-start | bytes 3145732
  132.0 5.3 %copy-start.9 = (f32[1024,256]{0,1:T(8,128)S(1)}, f32[1024,256]{0,1:T(8,128)}, u32[]{:S(2)}) copy-start(f32[1024,256]{0,1:T(8,128)} %all-reduce.7.cloned.1.call-done) | copy-start | bytes 3145732
  139.8 119.7 %all-reduce.9.cloned.1.call-start = ((), (), s32[]{:S(2)}) async-start(), calls=%async_computation.2 | async-start | bytes 2097152 | tf_op jit(solution)/shard_map/psum | solution.py:49
  259.5 2.9 %copy-start.2 = (bf16[1024,1024]{1,0:T(8,128)(2,1)S(1)}, bf16[1024,1024]{1,0:T(8,128)(2,1)}, u32[]{:S(2)}) copy-start(bf16[1024,1024]{1,0:T(8,128)(2,1)} %convolution_convert_fusion) | copy-start | bytes 6291460
  259.5 2.9 %copy-start.6 = (f32[1024,256]{0,1:T(8,128)S(1)}, f32[1024,256]{0,1:T(8,128)}, u32[]{:S(2)}) copy-start(f32[1024,256]{0,1:T(8,128)} %fusion.2) | copy-start | bytes 3145732
  259.5 2.9 %copy-start.7 = (f32[1024,256]{0,1:T(8,128)S(1)}, f32[1024,256]{0,1:T(8,128)}, u32[]{:S(2)}) copy-start(f32[1024,256]{0,1:T(8,128)} %all-reduce.11.cloned.1.call-done) | copy-start | bytes 3145732
  263.5 1.0 copy-start.3
  264.5 4.5 %copy-start.8 = (f32[1024,256]{1,0:T(8,128)S(1)}, f32[1024,256]{1,0:T(8,128)}, u32[]{:S(2)}) copy-start(f32[1024,256]{1,0:T(8,128)} %all-reduce.9.cloned.1.call-done) | copy-start | bytes 3145732
  266.3 2.7 copy-start.1
  266.3 2.7 copy-start.4
Sparse Core Ops, SparseCore 0:
  12.1 81.0 all-reduce.4
  96.1 35.8 all-reduce.6
  139.9 36.7 all-reduce.10
  180.7 78.7 all-reduce.8
where the time goes:
time: 278 us; the launch traced here: 277 us
  waiting for transfers between devices  204 us (73%)
  matrix products  34.6 us (12%)
  between operations  14.6 us (5%)
  local copies, waits for them, and re-layouts  12.2 us (4%)
  other arithmetic  11.5 us (4%)
    psum x2, waiting for transfers between devices, shards(): consensus = soft_shrink(lax.psum(q, 'samp') / n_samp)  132 us
    psum x2, waiting for transfers between devices, shards(): total = lax.psum(p, 'feat')  71.6 us
    dot_general x7, matrix products, dot(): return jnp.dot(a, b, preferred_element_type=f32)  21.5 us
    unnamed x31, local copies, waits for them, and re-layouts  12.2 us
    dot_general x1, matrix products, shards(): lax.dot_general(data, inverse.astype(bf16), (((0,), (0,)), ((), ())), pre...  10.7 us
  transfers between devices with their start and end apart: 4, of which 4 were waited for; matrix products, arithmetic and copies ran while one was open for 12% of the time, Pallas kernels for 0%

commit v1 on v0

v1 whole, which is shorter than its diff:
```python
import jax
import jax.numpy as jnp
from jax import lax
from jax.experimental import pallas as pl
from jax.experimental.pallas import tpu as pltpu
from jax.sharding import PartitionSpec as P

ITERS = 2
LANES = 128
BLOCK = 256
HALVES = 2
huber_width = 0.5
shrink_level = 0.1
f32 = jnp.float32
bf16 = jnp.bfloat16


def dot(a, b):
    return jnp.dot(a, b, preferred_element_type=f32)


def split(value):
    high = value.astype(bf16)
    low = (value - high.astype(f32)).astype(bf16)
    return jnp.concatenate([high, low], axis=1)


def joined_halves(value):
    return value[:, :LANES] + value[:, LANES:]


def soft_shrink(values):
    return values - jnp.clip(values, -shrink_level, shrink_level)


def huber_prox(values, weight):
    limit = huber_width * (1.0 + weight)
    shift = jnp.where(values > 0.0, weight * huber_width, -weight * huber_width)
    return jnp.where(jnp.abs(values) <= limit, values * (1.0 / (1.0 + weight)), values - shift)


def all_reduce(buf, rec, out, send, recv, axis, order, base, rows):
    index = lax.axis_index(axis)
    off, length, at, slot = base, rows, base, 0
    path = []
    for k, bit in enumerate(order):
        side = (index // (1 << bit)) % 2
        peer = index + (1 - 2 * side) * (1 << bit)
        if k < len(order) - 1:
            half = length // 2
            keep = off + side * half
            give = off + (1 - side) * half
            path.append((peer, off, length))
        else:
            half, keep, give = length, off, off
        if not isinstance(keep, int):
            keep, give = pl.multiple_of(keep, 8), pl.multiple_of(give, 8)
        copy = pltpu.make_async_remote_copy(
            src_ref=buf.at[pl.ds(give, half)],
            dst_ref=rec.at[pl.ds(at, half)],
            send_sem=send.at[slot],
            recv_sem=recv.at[slot],
            device_id={axis: peer},
            device_id_type=pl.DeviceIdType.MESH,
        )
        copy.start()
        yield
        copy.wait()
        target = buf if k < len(order) - 1 else out
        target[pl.ds(keep, half)] = buf[pl.ds(keep, half)] + rec[pl.ds(at, half)]
        off, length, at, slot = keep, half, at + half, slot + 1
    for peer, parent, extent in reversed(path):
        copy = pltpu.make_async_remote_copy(
            src_ref=out.at[pl.ds(off, length)],
            dst_ref=out.at[pl.ds(off, length)],
            send_sem=send.at[slot],
            recv_sem=recv.at[slot],
            device_id={axis: peer},
            device_id_type=pl.DeviceIdType.MESH,
        )
        copy.start()
        yield
        copy.wait()
        off, length, slot = parent, extent, slot + 1


def kernel(n_samp, n_feat, *refs):
    (a_ref, b_ref, x_ref, u_ref, y_ref, v_ref, nx_ref, nu_ref, ny_ref, nv_ref,
     q_ref, p_ref, sbuf, srec, sout, fbuf, frec, fout, at_ref, gram_ref, g16_ref, e16_ref, map_ref,
     ahead_ref, start_ref, s_send, s_recv, f_send, f_recv) = refs
    rows, cols = a_ref.shape
    chunks = b_ref.shape[1] // LANES
    s_bits = list(range(n_samp.bit_length() - 1))
    f_bits = list(range(n_feat.bit_length() - 1))

    barrier = pltpu.get_barrier_semaphore()
    for axis, bits in (("samp", s_bits), ("feat", f_bits)):
        index = lax.axis_index(axis)
        for bit in bits:
            side = (index // (1 << bit)) % 2
            pl.semaphore_signal(
                barrier,
                inc=1,
                device_id={axis: index + (1 - 2 * side) * (1 << bit)},
                device_id_type=pl.DeviceIdType.MESH,
            )

    lanes = [slice(c * LANES, (c + 1) * LANES) for c in range(chunks)]
    for c in range(chunks):
        q = x_ref[:, lanes[c]] + u_ref[:, lanes[c]]
        q_ref[c] = q
        sbuf[0, c] = q
        p = y_ref[:, lanes[c]] + v_ref[:, lanes[c]]
        p_ref[c] = p
        fbuf[0, c] = p
    pl.semaphore_wait(barrier, len(s_bits) + len(f_bits))

    def samp_unit(it, c, h):
        n = cols // HALVES
        return all_reduce(
            sbuf.at[it, c], srec.at[it, c], sout.at[it, c], s_send.at[it, c, h], s_recv.at[it, c, h],
            "samp", s_bits, h * n, n,
        )

    def feat_unit(it, c):
        return all_reduce(
            fbuf.at[it, c], frec.at[it, c], fout.at[it, c], f_send.at[it, c], f_recv.at[it, c],
            "feat", f_bits, 0, rows,
        )

    state = {}

    def blocks(lo, hi, body):
        def step(i, carry):
            body(pl.multiple_of(i * BLOCK, BLOCK))
            return carry

        lax.fori_loop(lo, hi, step, 0)

    def gram_block(i):
        part = a_ref[pl.ds(i, BLOCK), :]
        g = lax.dot_general(part, a_ref[...], (((1,), (1,)), ((), ())), preferred_element_type=f32)
        gram_ref[pl.ds(i, BLOCK), :] = g
        g16_ref[pl.ds(i, BLOCK), :] = g.astype(bf16)

    def diagonal(i):
        row = lax.broadcasted_iota(jnp.int32, (BLOCK, rows), 0) + i
        col = lax.broadcasted_iota(jnp.int32, (BLOCK, rows), 1)
        return row == col

    def scales():
        total = jnp.zeros((1, cols), f32)
        for i in range(0, rows, BLOCK):
            part = a_ref[i:i + BLOCK, :].astype(f32)
            total = total + jnp.sum(part * part, axis=0, keepdims=True)
        factor = 1.0 / (1.0 + 2.0 * jnp.sum(total, axis=1, keepdims=True) / rows)
        state["a"] = 2.0 * factor - factor * factor
        state["b"] = factor * factor

    def flip():
        for i in range(0, rows, BLOCK):
            at_ref[:, i:i + BLOCK] = a_ref[i:i + BLOCK, :].T

    def inner_block(i):
        a, b = state["a"], state["b"]
        square = dot(g16_ref[pl.ds(i, BLOCK), :], g16_ref[...])
        inner = (b - a) * gram_ref[pl.ds(i, BLOCK), :] + b * square
        gram_ref[pl.ds(i, BLOCK), :] = inner
        e16_ref[pl.ds(i, BLOCK), :] = (inner + jnp.where(diagonal(i), 2.0 - a, 0.0)).astype(bf16)

    def rest_block(i):
        a, b = state["a"], state["b"]
        gram_ref[pl.ds(i, BLOCK), :] = a * gram_ref[pl.ds(i, BLOCK), :] - b * dot(
            g16_ref[pl.ds(i, BLOCK), :], e16_ref[...]
        )

    def map_block(i):
        a = state["a"]
        part = at_ref[pl.ds(i, BLOCK), :]
        made = a * (2.0 - a) * part.astype(f32) + dot(part, e16_ref[...])
        map_ref[pl.ds(i, BLOCK), :] = made.astype(bf16)

    def narrow():
        e16_ref[...] = gram_ref[...].astype(bf16)

    n_blocks = rows // BLOCK
    c_blocks = cols // BLOCK
    tasks = [scales, flip]
    for body, count in ((gram_block, n_blocks), (inner_block, n_blocks), (rest_block, n_blocks), (None, 0), (map_block, c_blocks)):
        if body is None:
            tasks.append(narrow)
            continue
        middle = count // 2
        tasks.append(lambda body=body, middle=middle: blocks(0, middle, body))
        tasks.append(lambda body=body, middle=middle, count=count: blocks(middle, count, body))

    def spare():
        if tasks:
            tasks.pop(0)()

    def local(it, c):
        last = it == ITERS - 1
        cons = soft_shrink(sout[it, c] * (1.0 / n_samp))
        dual = q_ref[c] - cons
        start = cons - dual
        if last:
            nu_ref[:, lanes[c]] = dual
            start_ref[c] = start
        else:
            q_ref[c] = cons
        total = fout[it, c]
        goal = b_ref[:, lanes[c]]
        corr = (goal + huber_prox(total - goal, float(n_feat)) - total) * (1.0 / n_feat)
        if last:
            nv_ref[:, lanes[c]] = -corr
        ahead = dot(a_ref[...], start.astype(bf16))
        ahead_ref[c] = ahead
        residual = ahead - (p_ref[c] + 2.0 * corr)
        if not last:
            p_ref[c] = corr
        back = joined_halves(dot(map_ref[...], split(residual)))
        if last:
            nx_ref[:, lanes[c]] = start_ref[c] - back
        else:
            q = q_ref[c] - back
            q_ref[c] = q
            sbuf[it + 1, c] = q
        yield
        partials = ahead_ref[c] - joined_halves(dot(a_ref[...], split(back)))
        if last:
            ny_ref[:, lanes[c]] = partials
        else:
            p = partials - p_ref[c]
            p_ref[c] = p
            fbuf[it + 1, c] = p
        yield

    active = []
    turn = 0

    def launch(it, c, kind, first):
        if kind == "samp":
            for h in range(HALVES):
                gen = samp_unit(it, c, h)
                next(gen)
                active.append([first + h, gen, it, c])
        else:
            gen = feat_unit(it, c)
            next(gen)
            active.append([first, gen, it, c])

    for c in range(chunks):
        launch(0, c, "feat", c * HALVES)
        launch(0, c, "samp", c * HALVES)
    done = set()
    while active:
        turn += 1
        finished = []
        for unit in list(active):
            if unit[0] < turn:
                spare()
                if next(unit[1], "end") == "end":
                    active.remove(unit)
                    finished.append((unit[2], unit[3]))
        for it, c in sorted(set(finished)):
            if any(unit[2] == it and unit[3] == c for unit in active):
                continue
            while tasks:
                spare()
            step = local(it, c)
            next(step)
            if it + 1 < ITERS:
                launch(it + 1, c, "samp", turn)
            next(step)
            if it + 1 < ITERS:
                launch(it + 1, c, "feat", turn)


def shards(n_samp, n_feat, data, targets, tile_x, x_dual, tile_y, y_dual):
    rows, cols = data.shape
    width = targets.shape[1]
    chunks = width // LANES
    s_slots = 2 * (n_samp.bit_length() - 1) - 1
    f_slots = 2 * (n_feat.bit_length() - 1) - 1
    vmem = pl.BlockSpec(memory_space=pltpu.VMEM)
    outs = pl.pallas_call(
        lambda *refs: kernel(n_samp, n_feat, *refs),
        out_shape=(
            jax.ShapeDtypeStruct((cols, width), f32),
            jax.ShapeDtypeStruct((cols, width), f32),
            jax.ShapeDtypeStruct((rows, width), f32),
            jax.ShapeDtypeStruct((rows, width), f32),
        ),
        in_specs=[vmem] * 6,
        out_specs=(vmem,) * 4,
        scratch_shapes=[
            pltpu.VMEM((chunks, cols, LANES), f32),
            pltpu.VMEM((chunks, rows, LANES), f32),
            pltpu.VMEM((ITERS, chunks, cols, LANES), f32),
            pltpu.VMEM((ITERS, chunks, cols, LANES), f32),
            pltpu.VMEM((ITERS, chunks, cols, LANES), f32),
            pltpu.VMEM((ITERS, chunks, rows, LANES), f32),
            pltpu.VMEM((ITERS, chunks, rows, LANES), f32),
            pltpu.VMEM((ITERS, chunks, rows, LANES), f32),
            pltpu.VMEM((cols, rows), bf16),
            pltpu.VMEM((rows, rows), f32),
            pltpu.VMEM((rows, rows), bf16),
            pltpu.VMEM((rows, rows), bf16),
            pltpu.VMEM((cols, rows), bf16),
            pltpu.VMEM((chunks, rows, LANES), f32),
            pltpu.VMEM((chunks, cols, LANES), f32),
            pltpu.SemaphoreType.DMA((ITERS, chunks, HALVES, s_slots)),
            pltpu.SemaphoreType.DMA((ITERS, chunks, HALVES, s_slots)),
            pltpu.SemaphoreType.DMA((ITERS, chunks, f_slots)),
            pltpu.SemaphoreType.DMA((ITERS, chunks, f_slots)),
        ],
        compiler_params=pltpu.CompilerParams(
            collective_id=0, has_side_effects=True, vmem_limit_bytes=60 * 1024 * 1024
        ),
    )(data, targets, tile_x[0], x_dual[0], tile_y[0], y_dual[0])
    return tuple(out[None] for out in outs)


def solution(mesh):
    n_samp, n_feat = mesh.shape["samp"], mesh.shape["feat"]
    return jax.shard_map(
        lambda *args: shards(n_samp, n_feat, *args),
        mesh=mesh,
        in_specs=(
            P("samp", "feat"),
            P("samp", None),
            P("samp", "feat", None),
            P("samp", "feat", None),
            P("feat", "samp", None),
            P("feat", "samp", None),
        ),
        out_specs=(
            P("samp", "feat", None),
            P("samp", "feat", None),
            P("feat", "samp", None),
            P("feat", "samp", None),
        ),
        check_vma=False,
    )
```

time: 278 us -> 93 us (0.33)
  waiting for transfers between devices: 204 us -> 0 us
  Pallas kernels: 0 us -> 86.9 us
  matrix products: 34.6 us -> 0 us
  between operations: 14.6 us -> 0.66 us
  other arithmetic: 11.5 us -> 0 us
  local copies, waits for them, and re-layouts: 12.2 us -> 5.33 us
    psum x4 -> x0, waiting for transfers between devices: 204 us -> none  [the longest x2 132 us: shards(): consensus = soft_shrink(lax.psum(q, 'samp') / n_samp)]
    pallas_call x0 -> x1, Pallas kernels: none -> 86.9 us  [shards(): pl.pallas_call(lambda *refs: kernel(n_samp, n_feat, *refs), out_shape=(ja...]
    dot_general x9 -> x0, matrix products: 34.6 us -> none  [the longest x7 21.5 us: dot(): return jnp.dot(a, b, preferred_element_type=f32)]
    unnamed x31 -> x10, local copies, waits for them, and re-layouts: 12.2 us -> 5.33 us
    add x2 -> x0, other arithmetic: 5.2 us -> none  [the longest x1 2.72 us: shards(): q = tile_x[0] + x_dual[0]]
  transfers between devices with their start and end apart: 4 -> 0, of which waited for: 4 -> 0; matrix products, arithmetic and copies ran while one was open for 12% -> 0% of each run, Pallas kernels for 0% -> 0%
where the time goes in v1:
time: 93 us; the launch traced here: 92.9 us
  Pallas kernels  86.9 us (93%)
  local copies, waits for them, and re-layouts  5.33 us (6%)
    pallas_call x1, Pallas kernels, shards(): pl.pallas_call(lambda *refs: kernel(n_samp, n_feat, *refs), out_shape=(ja...  86.9 us
    unnamed x10, local copies, waits for them, and re-layouts  5.33 us

profile of v1, /device:TPU:0, one launch (start us, length us, event | category | flops | bytes accessed | tf_op | source)
XLA Modules:
  0.0 92.9 jit_solution(2001916212232768833)
XLA Ops:
  0.6 86.9 %shard_map.93 = (f32[1024,256]{1,0:T(8,128)}, f32[1024,256]{1,0:T(8,128)}, f32[1024,256]{1,0:T(8,128)}, f32[1024,256]{1,0:T(8,128)}) custom-call(bf16[1024,1024]{1,0:T(8,128)(2,1)} %refs_0_.1, f32[1024,256]{1,0:T(8,128)} %refs_1_.1, f32[1024,256]{1,0:T(8,128)} %bitcast.8, f32[1024,256]{1,0:T(8,128)} %bitcast.9, f32[1024,256]{1,0:T(8,128)} %bitcast.10, ...), custom_call_target="tpu_custom_call" | custom-call | tf_op jit(solution)/shard_map/pallas_call | solution.py:286
  87.5 0.0 copy-start.2
  87.5 0.0 copy-start.1
  87.6 2.4 %copy.14 = f32[1,1024,256]{2,1,0:T(8,128)} copy(f32[1,1024,256]{2,1,0:T(8,128)} %bitcast.15) | data formatting | bytes 2097152
  90.0 0.0 copy-done.2
  90.0 0.0 copy-start
  90.0 1.0 %copy.15 = f32[1,1024,256]{2,1,0:T(8,128)} copy(f32[1,1024,256]{2,1,0:T(8,128)S(1)} %bitcast.14) | data formatting | bytes 2097152
  90.9 0.0 copy-done.1
  90.9 1.0 %copy.16 = f32[1,1024,256]{2,1,0:T(8,128)} copy(f32[1,1024,256]{2,1,0:T(8,128)S(1)} %bitcast.13) | data formatting | bytes 2097152
  91.9 0.0 copy-done
  91.9 1.0 %copy.17 = f32[1,1024,256]{2,1,0:T(8,128)} copy(f32[1,1024,256]{2,1,0:T(8,128)S(1)} %bitcast.12) | data formatting | bytes 2097152
Async XLA Ops:
  87.5 2.4 %copy-start.2 = (f32[1024,256]{1,0:T(8,128)S(1)}, f32[1024,256]{1,0:T(8,128)}, u32[]{:S(2)}) copy-start(f32[1024,256]{1,0:T(8,128)} %get-tuple-element.9) | copy-start | bytes 3145732
  87.5 3.4 %copy-start.1 = (f32[1024,256]{1,0:T(8,128)S(1)}, f32[1024,256]{1,0:T(8,128)}, u32[]{:S(2)}) copy-start(f32[1024,256]{1,0:T(8,128)} %get-tuple-element.10) | copy-start | bytes 3145732
  90.0 1.9 %copy-start = (f32[1024,256]{1,0:T(8,128)S(1)}, f32[1024,256]{1,0:T(8,128)}, u32[]{:S(2)}) copy-start(f32[1024,256]{1,0:T(8,128)} %get-tuple-element.11) | copy-start | bytes 3145732

commit v2 on v1

--- a/solution.py
+++ b/solution.py
@@ -8,7 +8,7 @@
 ITERS = 2
 LANES = 128
 BLOCK = 256
-HALVES = 2
+PIECES = 4
 huber_width = 0.5
 shrink_level = 0.1
 f32 = jnp.float32
@@ -91,6 +91,7 @@
     rows, cols = a_ref.shape
     chunks = b_ref.shape[1] // LANES
     s_bits = list(range(n_samp.bit_length() - 1))
+    s_turned = s_bits[1:2] + s_bits[:1] + s_bits[2:]
     f_bits = list(range(n_feat.bit_length() - 1))
 
     barrier = pltpu.get_barrier_semaphore()
@@ -116,10 +117,10 @@
     pl.semaphore_wait(barrier, len(s_bits) + len(f_bits))
 
     def samp_unit(it, c, h):
-        n = cols // HALVES
+        n = cols // PIECES
         return all_reduce(
             sbuf.at[it, c], srec.at[it, c], sout.at[it, c], s_send.at[it, c, h], s_recv.at[it, c, h],
-            "samp", s_bits, h * n, n,
+            "samp", s_turned if h == 0 else s_bits, h * n, n,
         )
 
     def feat_unit(it, c):
@@ -218,6 +219,7 @@
         residual = ahead - (p_ref[c] + 2.0 * corr)
         if not last:
             p_ref[c] = corr
+        yield None
         back = joined_halves(dot(map_ref[...], split(residual)))
         if last:
             nx_ref[:, lanes[c]] = start_ref[c] - back
@@ -225,7 +227,7 @@
             q = q_ref[c] - back
             q_ref[c] = q
             sbuf[it + 1, c] = q
-        yield
+        yield None if last else "samp"
         partials = ahead_ref[c] - joined_halves(dot(a_ref[...], split(back)))
         if last:
             ny_ref[:, lanes[c]] = partials
@@ -233,14 +235,14 @@
             p = partials - p_ref[c]
             p_ref[c] = p
             fbuf[it + 1, c] = p
-        yield
+        yield None if last else "feat"
 
     active = []
     turn = 0
 
     def launch(it, c, kind, first):
         if kind == "samp":
-            for h in range(HALVES):
+            for h in range(PIECES):
                 gen = samp_unit(it, c, h)
                 next(gen)
                 active.append([first + h, gen, it, c])
@@ -250,30 +252,36 @@
             active.append([first, gen, it, c])
 
     for c in range(chunks):
-        launch(0, c, "feat", c * HALVES)
-        launch(0, c, "samp", c * HALVES)
-    done = set()
-    while active:
+        launch(0, c, "feat", c * PIECES)
+        launch(0, c, "samp", c * PIECES)
+    working = []
+    count = 0
+    while active or working:
         turn += 1
-        finished = []
+        finished = set()
         for unit in list(active):
             if unit[0] < turn:
-                spare()
+                count += 1
+                if count % 2 == 0:
+                    spare()
                 if next(unit[1], "end") == "end":
                     active.remove(unit)
-                    finished.append((unit[2], unit[3]))
-        for it, c in sorted(set(finished)):
+                    finished.add((unit[2], unit[3]))
+        for work in list(working):
+            it, c, step = work
+            kind = next(step, "end")
+            if kind == "end":
+                working.remove(work)
+            elif kind is not None:
+                launch(it + 1, c, kind, turn)
+        for it, c in sorted(finished):
             if any(unit[2] == it and unit[3] == c for unit in active):
                 continue
             while tasks:
                 spare()
             step = local(it, c)
             next(step)
-            if it + 1 < ITERS:
-                launch(it + 1, c, "samp", turn)
-            next(step)
-            if it + 1 < ITERS:
-                launch(it + 1, c, "feat", turn)
+            working.append((it, c, step))
 
 
 def shards(n_samp, n_feat, data, targets, tile_x, x_dual, tile_y, y_dual):
@@ -309,8 +317,8 @@
             pltpu.VMEM((cols, rows), bf16),
             pltpu.VMEM((chunks, rows, LANES), f32),
             pltpu.VMEM((chunks, cols, LANES), f32),
-            pltpu.SemaphoreType.DMA((ITERS, chunks, HALVES, s_slots)),
-            pltpu.SemaphoreType.DMA((ITERS, chunks, HALVES, s_slots)),
+            pltpu.SemaphoreType.DMA((ITERS, chunks, PIECES, s_slots)),
+            pltpu.SemaphoreType.DMA((ITERS, chunks, PIECES, s_slots)),
             pltpu.SemaphoreType.DMA((ITERS, chunks, f_slots)),
             pltpu.SemaphoreType.DMA((ITERS, chunks, f_slots)),
         ],

time: 93 us -> 109 us (1.17)
  Pallas kernels: 86.9 us -> 103 us
    pallas_call x1, Pallas kernels: 86.9 us -> 103 us  [shards(): pl.pallas_call(lambda *refs: kernel(n_samp, n_feat, *refs), out_shape=(ja...]
where the time goes in v2:
time: 109 us
  Pallas kernels  103 us (94%)
  local copies, waits for them, and re-layouts  5.33 us (5%)
    pallas_call x1, Pallas kernels, shards(): pl.pallas_call(lambda *refs: kernel(n_samp, n_feat, *refs), out_shape=(ja...  103 us
    unnamed x10, local copies, waits for them, and re-layouts  5.33 us

profile of v2, /device:TPU:0, one launch (start us, length us, event | category | flops | bytes accessed | tf_op | source)
XLA Modules:
  0.0 109.1 jit_solution(4749472914910507695)
XLA Ops:
  0.6 103.1 %shard_map.93 = (f32[1024,256]{1,0:T(8,128)}, f32[1024,256]{1,0:T(8,128)}, f32[1024,256]{1,0:T(8,128)}, f32[1024,256]{1,0:T(8,128)}) custom-call(bf16[1024,1024]{1,0:T(8,128)(2,1)} %refs_0_.1, f32[1024,256]{1,0:T(8,128)} %refs_1_.1, f32[1024,256]{1,0:T(8,128)} %bitcast.8, f32[1024,256]{1,0:T(8,128)} %bitcast.9, f32[1024,256]{1,0:T(8,128)} %bitcast.10, ...), custom_call_target="tpu_custom_call" | custom-call | tf_op jit(solution)/shard_map/pallas_call | solution.py:294
  103.8 0.0 copy-start.2
  103.8 0.0 copy-start.1
  103.8 2.4 %copy.14 = f32[1,1024,256]{2,1,0:T(8,128)} copy(f32[1,1024,256]{2,1,0:T(8,128)} %bitcast.15) | data formatting | bytes 2097152
  106.2 0.0 copy-done.2
  106.2 0.0 copy-start
  106.2 1.0 copy.15
  107.2 0.0 copy-done.1
  107.2 1.0 copy.16
  108.2 0.0 copy-done
  108.2 1.0 copy.17
Async XLA Ops:
  103.8 2.4 %copy-start.2 = (f32[1024,256]{1,0:T(8,128)S(1)}, f32[1024,256]{1,0:T(8,128)}, u32[]{:S(2)}) copy-start(f32[1024,256]{1,0:T(8,128)} %get-tuple-element.9) | copy-start | bytes 3145732
  103.8 3.4 %copy-start.1 = (f32[1024,256]{1,0:T(8,128)S(1)}, f32[1024,256]{1,0:T(8,128)}, u32[]{:S(2)}) copy-start(f32[1024,256]{1,0:T(8,128)} %get-tuple-element.10) | copy-start | bytes 3145732
  106.2 1.9 %copy-start = (f32[1024,256]{1,0:T(8,128)S(1)}, f32[1024,256]{1,0:T(8,128)}, u32[]{:S(2)}) copy-start(f32[1024,256]{1,0:T(8,128)} %get-tuple-element.11) | copy-start | bytes 3145732
